TPU v7x, 32 devices: a whole 2x2x4 slice. The times are simulated.
32 devices in a mesh: grp: 2 (over y), seg: 4 (over z), tm: 2 (over x), rep: 2 (over core).
Axes of the slice: x: 2, y: 2, z: 4, core: 2. Of those that a mesh axis runs over, the one named last changes fastest.
Arguments:
- series: bfloat16 [3072, 2, 16, 128], P(('grp', 'seg'), 'rep', 'tm'), parts along dimension 0, may hold values from -6 to 6
- cotangent: bfloat16 [3072, 2, 16, 128], P(('grp', 'seg'), 'rep', 'tm'), parts along dimension 0, may hold values from -6 to 6
- w_filter: bfloat16 [2, 128, 128], replicated, may hold values from -0.375 to 0.375
- w_gate: bfloat16 [2, 128, 128], replicated, may hold values from -0.375 to 0.375
- b_filter: float32 [128], replicated, may hold values from -3 to 3
- b_gate: float32 [128], replicated, may hold values from -3 to 3
- w_diff: bfloat16 [3, 128, 128], replicated, may hold values from -0.5 to 0.5
- b_diff: float32 [128], replicated, may hold values from -3 to 3
- tile_row: int32 [8, 9], P(('grp', 'seg')), parts along dimension 0, may hold values from 0 to 2, as said below
- tile_col: int32 [8, 9], P(('grp', 'seg')), parts along dimension 0, may hold values from 0 to 5, as said below
- tile_val: bfloat16 [8, 9, 128, 128], P(('grp', 'seg')), parts along dimension 0, may hold values from -0.5 to 0.5
- send_nodes: int32 [8, 3, 128], P(('grp', 'seg')), parts along dimension 0, may hold values from 0 to 383
- send_count: int32 [8, 3], P(('grp', 'seg')), parts along dimension 0, may hold values from 0 to 128, as said below
Outputs:
- output: bfloat16 [3072, 2, 16, 128], P(('grp', 'seg'), 'rep', 'tm'), parts along dimension 0
- grad_series: bfloat16 [3072, 2, 16, 128], P(('grp', 'seg'), 'rep', 'tm'), parts along dimension 0
- grad_w_filter: float32 [4, 128, 128], P('grp'), parts along dimension 0
- grad_w_gate: float32 [4, 128, 128], P('grp'), parts along dimension 0
- grad_b_filter: float32 [256], P('grp'), parts along dimension 0
- grad_b_gate: float32 [256], P('grp'), parts along dimension 0
- grad_w_diff: float32 [6, 128, 128], P('grp'), parts along dimension 0
- grad_b_diff: float32 [256], P('grp'), parts along dimension 0
There are 2 independent parts, one for each index of `grp`. A program takes and returns all parts, laid end to end along the dimension named above; an argument that names none is the same for every part. Nothing has to cross between parts.
Inputs may be any that keep to these rules, and one draw needn't show every extreme that they name: The first 3 tiles of each partition have tile_row 0, 1, ..., 2 in order. The first 3 tiles of each partition have tile_col 0, ..., 2 and the next 3 have tile_col 3, ..., 5, in order. `send_count`: list j of partition q is read by partition (q - d_j) mod 4; list 0 of every partition has 128 live entries.
All inputs are finite; a program needn't handle non-finite values.
Results may differ from a plain program's by a relative error of at most 0.0062.
Values may be sent and summed in bfloat16 or wider, within the bound.
A program may use at most 128 MiB of HBM per device.

v0:
```python
import math

import jax
import jax.numpy as jnp
from jax import lax
from jax.sharding import PartitionSpec as P

DILATION_FRAMES = 8


neighbour_steps = (1, -1, 2)


def passed_along(value, axis, steps):
    count = lax.axis_size(axis)
    pairs = [(source, (source + steps) % count) for source in range(count)]
    return lax.ppermute(value, axis, pairs)


def passed_along_2(array, axis, by):
    count = lax.axis_size(axis)
    pairs = [(i, i + by) for i in range(count) if 0 <= i + by < count]
    return lax.ppermute(array, axis, pairs)


def linear_map(inputs, weight):
    return jnp.dot(inputs, weight, preferred_element_type=jnp.float32)


def linear_back(inputs, weight):
    return lax.dot_general(
        inputs, weight, (((1,), (1,)), ((), ())), preferred_element_type=jnp.float32
    )


def outer_sum(left_rows, right_rows):
    return lax.dot_general(
        left_rows, right_rows, (((0,), (0,)), ((), ())), preferred_element_type=jnp.float32
    )


def pre_acts(prior_frames, current, w_filter, w_gate, b_filter, b_gate):
    channels = current.shape[-1]
    prev_rows = prior_frames.reshape(-1, channels)
    curr_rows = current.reshape(-1, channels)
    filter_pre = linear_map(prev_rows, w_filter[0]) + linear_map(curr_rows, w_filter[1]) + b_filter
    gate_pre = linear_map(prev_rows, w_gate[0]) + linear_map(curr_rows, w_gate[1]) + b_gate
    return (filter_pre, gate_pre)


def gated_units(filter_pre, gate_pre):
    return (jnp.tanh(filter_pre) * jax.nn.sigmoid(gate_pre)).astype(jnp.bfloat16)


def spread_tiles(source, row_list, col_list, tile_values, out_rows):
    tile_side = tile_values.shape[1]
    row_width = source.shape[1]
    source_blocks = source.reshape(-1, tile_side, row_width)
    picked = jnp.take(source_blocks, col_list, axis=0)
    products = jnp.einsum("kij,kjw->kiw", tile_values, picked, preferred_element_type=jnp.float32)
    block_ids = lax.broadcasted_iota(jnp.int32, (out_rows // tile_side, tile_values.shape[0]), 0)
    selector = (block_ids == row_list[None, :]).astype(jnp.float32)
    summed = jnp.einsum(
        "rk,kiw->riw",
        selector,
        products,
        precision=lax.Precision.HIGHEST,
        preferred_element_type=jnp.float32,
    )
    return summed.reshape(out_rows, row_width)


def gather_tiles(cotan, row_list, col_list, tile_values, out_rows):
    tile_side = tile_values.shape[1]
    row_width = cotan.shape[1]
    cotan_blocks = cotan.reshape(-1, tile_side, row_width)
    picked = jnp.take(cotan_blocks, row_list, axis=0)
    products = jnp.einsum("kji,kjw->kiw", tile_values, picked, preferred_element_type=jnp.float32)
    block_ids = lax.broadcasted_iota(jnp.int32, (out_rows // tile_side, tile_values.shape[0]), 0)
    selector = (block_ids == col_list[None, :]).astype(jnp.float32)
    summed = jnp.einsum(
        "rk,kiw->riw",
        selector,
        products,
        precision=lax.Precision.HIGHEST,
        preferred_element_type=jnp.float32,
    )
    return summed.reshape(out_rows, row_width)


def to_readers(packed):
    pieces = [
        passed_along(packed[neighbour], "seg", -offset)
        for neighbour, offset in enumerate(neighbour_steps)
    ]
    return jnp.stack(pieces)


def to_owners(partials):
    pieces = [
        passed_along(partials[neighbour], "seg", offset)
        for neighbour, offset in enumerate(neighbour_steps)
    ]
    return jnp.stack(pieces)


def on_device(
    series,
    cotangent,
    w_filter,
    w_gate,
    b_filter,
    b_gate,
    w_diff,
    b_diff,
    tile_row,
    tile_col,
    tile_val,
    send_nodes,
    send_count,
):
    nodes, batch, frame_series, channels = series.shape
    row_list = tile_row[0]
    col_list = tile_col[0]
    tile_values = tile_val[0]
    targets = send_nodes[0]
    list_count, capacity = targets.shape
    halo_rows = list_count * capacity
    flat_targets = targets.reshape(-1)
    live_mask = (
        lax.broadcasted_iota(jnp.int32, (list_count, capacity), 1) < send_count[0][:, None]
    ).astype(jnp.bfloat16)
    row_width = batch * frame_series * channels

    def pack_rows(field):
        picked = jnp.take(field, flat_targets, axis=0).reshape(list_count, capacity, field.shape[1])
        return picked * live_mask[:, :, None]

    def return_rows(received):
        masked = received.astype(jnp.float32) * live_mask[:, :, None].astype(jnp.float32)
        empty = jnp.zeros((nodes, received.shape[2]), jnp.float32)
        return empty.at[flat_targets].add(masked.reshape(halo_rows, -1))

    earlier = passed_along_2(series, "tm", 1)
    extended = jnp.concatenate([earlier, series], axis=2)
    prior_frames = extended[:, :, :frame_series]
    filter_pre, gate_pre = pre_acts(prior_frames, series, w_filter, w_gate, b_filter, b_gate)
    hidden = gated_units(filter_pre, gate_pre)
    hidden_flat = hidden.reshape(nodes, row_width)
    halo_first = to_readers(pack_rows(hidden_flat)).reshape(halo_rows, row_width)
    hop_one = spread_tiles(
        jnp.concatenate([hidden_flat, halo_first], axis=0), row_list, col_list, tile_values, nodes
    ).astype(jnp.bfloat16)
    halo_second = to_readers(pack_rows(hop_one)).reshape(halo_rows, row_width)
    hop_two = spread_tiles(
        jnp.concatenate([hop_one, halo_second], axis=0), row_list, col_list, tile_values, nodes
    ).astype(jnp.bfloat16)
    one_rows = hop_one.reshape(-1, channels)
    two_rows = hop_two.reshape(-1, channels)
    diffusion_out = (
        linear_map(hidden, w_diff[0])
        + linear_map(one_rows, w_diff[1])
        + linear_map(two_rows, w_diff[2])
        + b_diff
    )
    output = (
        (series.reshape(-1, channels).astype(jnp.float32) + diffusion_out)
        .astype(jnp.bfloat16)
        .reshape(series.shape)
    )
    grad_rows = cotangent.reshape(-1, channels)
    bias_diff = jnp.sum(grad_rows.astype(jnp.float32), axis=0)
    weight_diff = jnp.stack(
        [
            outer_sum(hidden, grad_rows),
            outer_sum(one_rows, grad_rows),
            outer_sum(two_rows, grad_rows),
        ]
    )
    up_two = linear_back(grad_rows, w_diff[2]).astype(jnp.bfloat16).reshape(nodes, row_width)
    back_two = gather_tiles(up_two, row_list, col_list, tile_values, nodes + halo_rows)
    sent_two = back_two[nodes:].astype(jnp.bfloat16).reshape(list_count, capacity, row_width)
    transposed_two = back_two[:nodes] + return_rows(to_owners(sent_two))
    up_one = (
        (linear_back(grad_rows, w_diff[1]) + transposed_two.reshape(-1, channels))
        .astype(jnp.bfloat16)
        .reshape(nodes, row_width)
    )
    back_one = gather_tiles(up_one, row_list, col_list, tile_values, nodes + halo_rows)
    sent_one = back_one[nodes:].astype(jnp.bfloat16).reshape(list_count, capacity, row_width)
    transposed_one = back_one[:nodes] + return_rows(to_owners(sent_one))
    grad_hidden = linear_back(grad_rows, w_diff[0]) + transposed_one.reshape(-1, channels)
    act_filter = jnp.tanh(filter_pre)
    act_gate = jax.nn.sigmoid(gate_pre)
    grad_filter = (grad_hidden * act_gate * (1.0 - act_filter * act_filter)).astype(jnp.bfloat16)
    grad_gate = (grad_hidden * act_filter * (act_gate * (1.0 - act_gate))).astype(jnp.bfloat16)
    prev_rows = prior_frames.reshape(-1, channels)
    curr_rows = series.reshape(-1, channels)
    weight_filter = jnp.stack(
        [outer_sum(prev_rows, grad_filter), outer_sum(curr_rows, grad_filter)]
    )
    bias_filter = jnp.sum(grad_filter.astype(jnp.float32), axis=0)
    weight_gate = jnp.stack([outer_sum(prev_rows, grad_gate), outer_sum(curr_rows, grad_gate)])
    bias_gate = jnp.sum(grad_gate.astype(jnp.float32), axis=0)
    lagged_series = (
        linear_back(grad_filter, w_filter[0]) + linear_back(grad_gate, w_gate[0])
    ).astype(jnp.bfloat16)
    lagged_series = lagged_series.reshape(nodes, batch, frame_series, channels)
    received_following = passed_along_2(lagged_series, "tm", -1)
    shifted_series = jnp.concatenate(
        [lagged_series[:, :, DILATION_FRAMES:], received_following], axis=2
    )
    grad_series = (
        (
            grad_rows.astype(jnp.float32)
            + linear_back(grad_filter, w_filter[1])
            + linear_back(grad_gate, w_gate[1])
            + shifted_series.reshape(-1, channels).astype(jnp.float32)
        )
        .astype(jnp.bfloat16)
        .reshape(series.shape)
    )
    grad_scale = 1.0 / math.sqrt(
        nodes
        * batch
        * frame_series
        * lax.axis_size("seg")
        * lax.axis_size("tm")
        * lax.axis_size("rep")
    )
    filter_total, gate_total, bias_filter_total, bias_gate_total, diff_total, bias_diff_total = (
        lax.psum(
            (weight_filter, weight_gate, bias_filter, bias_gate, weight_diff, bias_diff),
            ("seg", "tm", "rep"),
        )
    )
    return (
        output,
        grad_series,
        filter_total * grad_scale,
        gate_total * grad_scale,
        bias_filter_total * grad_scale,
        bias_gate_total * grad_scale,
        diff_total * grad_scale,
        bias_diff_total * grad_scale,
    )


def solution(mesh):
    in_specs = (
        P(("grp", "seg"), "rep", "tm", None),
        P(("grp", "seg"), "rep", "tm", None),
        P(),
        P(),
        P(),
        P(),
        P(),
        P(),
        P(("grp", "seg"), None),
        P(("grp", "seg"), None),
        P(("grp", "seg"), None, None, None),
        P(("grp", "seg"), None, None),
        P(("grp", "seg"), None),
    )
    out_specs = (
        P(("grp", "seg"), "rep", "tm", None),
        P(("grp", "seg"), "rep", "tm", None),
        P("grp", None, None),
        P("grp", None, None),
        P("grp"),
        P("grp"),
        P("grp", None, None),
        P("grp"),
    )
    return jax.shard_map(
        on_device, mesh=mesh, in_specs=in_specs, out_specs=out_specs, check_vma=False
    )
```

profile of v0, /device:TPU:0, one launch (start us, length us, event | category | flops | bytes accessed | tf_op | source)
XLA Modules:
  0.0 395.0 jit_solution(2179970105627740985)
XLA Ops:
  14.4 8.1 %copy.77 = f32[9,128,1024]{2,0,1:T(8,128)} copy(f32[9,128,1024]{1,2,0:T(8,128)} %fusion.30) | data formatting | bytes 9437184 | tf_op jit(solution)/shard_map/kji,kjw->kiw/dot_general | solution.py:78
  22.5 8.6 %fusion.124 = (bf16[6,128,1024]{2,0,1:T(8,128)(2,1)S(1)}, f32[6,128,1024]{2,0,1:T(8,128)}) fusion(f32[9,128,1024]{2,0,1:T(8,128)} %copy.77, s32[9]{0:T(128)S(1)} %bitcast.256), kind=kOutput, calls=%fused_computation.190 | convolution fusion | flops 85721144 | bytes 9437220 | tf_op jit(solution)/shard_map/rk,kiw->riw/dot_general | solution.py:81
  51.3 9.6 %collective-permute-done.9 = bf16[128,1024]{1,0:T(8,128)(2,1)} collective-permute-done((bf16[128,1024]{1,0:T(8,128)(2,1)S(1)}, bf16[128,1024]{1,0:T(8,128)(2,1)}, u32[]{:S(2)}, u32[]{:S(2)}) %collective-permute-start.9) | collective-permute-done | bytes 262176 | tf_op jit(solution)/shard_map/ppermute | solution.py:17
  62.1 6.3 %scatter_custom_fusion = f32[384,1024]{1,0:T(8,128)} fusion(f32[384,1024]{1,0:T(8,128)} %bitcast.233, s32[384]{0:T(512)S(1)} %fusion.111, bf16[384,1024]{1,0:T(8,128)(2,1)S(1)} %bitcast.236, f32[384]{0:T(512)S(1)} %get-tuple-element.76), kind=kCustom, calls=%fused_computation.56 | custom fusion | flops 1179648 | bytes 2361344 | tf_op jit(solution)/shard_map/scatter-add | solution.py:142
  77.6 4.9 %fusion.33 = f32[9,128,1024]{1,2,0:T(8,128)} fusion(bf16[9,128,1024]{2,1,0:T(8,128)(2,1)} %gather_fusion.5, pred[9]{0:T(512)(128)(4,1)} %copy-done.33, bf16[1,9,128,128]{3,2,1,0:T(8,128)(2,1)S(1)} %copy-done), kind=kOutput, calls=%fused_computation.46 | convolution fusion | flops 303169536 | bytes 7372809 | tf_op jit(solution)/shard_map/kji,kjw->kiw/dot_general | solution.py:78
  82.5 8.1 %copy.80 = f32[9,128,1024]{2,0,1:T(8,128)} copy(f32[9,128,1024]{1,2,0:T(8,128)} %fusion.33) | data formatting | bytes 9437184 | tf_op jit(solution)/shard_map/kji,kjw->kiw/dot_general | solution.py:78
  90.5 8.5 %fusion.125 = (bf16[6,128,1024]{2,0,1:T(8,128)(2,1)S(1)}, f32[6,128,1024]{2,0,1:T(8,128)S(1)}) fusion(f32[9,128,1024]{2,0,1:T(8,128)} %copy.80, s32[9]{0:T(128)S(1)} %bitcast.257), kind=kOutput, calls=%fused_computation.191 | convolution fusion | flops 85721144 | bytes 9437220 | tf_op jit(solution)/shard_map/rk,kiw->riw/dot_general | solution.py:81
  100.7 4.0 %collective-permute-start.11 = (bf16[128,1024]{1,0:T(8,128)(2,1)S(1)}, bf16[128,1024]{1,0:T(8,128)(2,1)S(1)}, u32[]{:S(2)}, u32[]{:S(2)}) collective-permute-start(bf16[128,1024]{1,0:T(8,128)(2,1)S(1)} %bitcast.245), channel_id=1, source_target_pairs={{0,12},{4,0},{8,4},{12,8},{1,13},{5,1},{9,5},{13,9},{2,14},{6,2},{... | collective-permute-start | bytes 786440 | tf_op jit(solution)/shard_map/ppermute | solution.py:17
  111.6 5.5 %collective-permute-done.11 = bf16[128,1024]{1,0:T(8,128)(2,1)S(1)} collective-permute-done((bf16[128,1024]{1,0:T(8,128)(2,1)S(1)}, bf16[128,1024]{1,0:T(8,128)(2,1)S(1)}, u32[]{:S(2)}, u32[]{:S(2)}) %collective-permute-start.11) | collective-permute-done | bytes 262176 | tf_op jit(solution)/shard_map/ppermute | solution.py:17
  117.1 8.1 %collective-permute-done.12 = bf16[128,1024]{1,0:T(8,128)(2,1)S(1)} collective-permute-done((bf16[128,1024]{1,0:T(8,128)(2,1)S(1)}, bf16[128,1024]{1,0:T(8,128)(2,1)S(1)}, u32[]{:S(2)}, u32[]{:S(2)}) %collective-permute-start.12) | collective-permute-done | bytes 262176 | tf_op jit(solution)/shard_map/ppermute | solution.py:17
  125.3 6.5 %scatter_custom_fusion.1 = f32[384,1024]{1,0:T(8,128)} fusion(f32[384,1024]{1,0:T(8,128)} %bitcast.234, s32[384]{0:T(512)} %copy-done.30, bf16[384,1024]{1,0:T(8,128)(2,1)S(1)} %bitcast.235, f32[384]{0:T(512)S(1)} %get-tuple-element.76), kind=kCustom, calls=%fused_computation.54 | custom fusion | flops 1179648 | bytes 2360832 | tf_op jit(solution)/shard_map/scatter-add | solution.py:142
  137.9 4.0 %convert_reduce_fusion.1 = (f32[128]{0:T(128)}, bf16[3072,128]{1,0:T(8,128)(2,1)}, f32[128]{0:T(128)}, bf16[3072,128]{1,0:T(8,128)(2,1)S(1)}, bf16[3072,128]{1,0:T(8,128)(2,1)}) fusion(f32[3072,128]{1,0:T(8,128)S(1)} %convolution_add_fusion.4, f32[3072,128]{1,0:T(8,128)S(1)} %fusion.8, f32[128]{0:T(128)S(1)} %copy-done.40, f32[3072,128]{1,0:T(8,128)S(1)} %copy-done.11, ...), kind=kOutput, calls=%fused_computation.59 | convolution fusion | flops 108920576 | bytes 7898624 | tf_op jit(solution)/shard_map/dot_general | solution.py:27
  149.6 30.8 %all-reduce = (f32[128]{0:T(128)}, f32[128]{0:T(128)}, f32[128]{0:T(128)}) all-reduce(f32[128]{0:T(128)} %get-tuple-element.61, f32[128]{0:T(128)} %get-tuple-element.57, f32[128]{0:T(128)S(1)} %copy-done.39), channel_id=1, replica_groups=mesh['grp'=2,'seg'=4,'tm'=2,'rep'=2] {'seg','tm','rep'}, use_global_device_ids=true, to_apply=%region_5.9 | all-reduce | flops 384 | bytes 3072 | tf_op jit(solution)/shard_map/psum | solution.py:232
  199.0 7.4 %collective-permute-done.3 = bf16[128,1024]{1,0:T(8,128)(2,1)S(1)} collective-permute-done((bf16[128,1024]{1,0:T(8,128)(2,1)S(1)}, bf16[128,1024]{1,0:T(8,128)(2,1)S(1)}, u32[]{:S(2)}, u32[]{:S(2)}) %collective-permute-start.3) | collective-permute-done | bytes 262176 | tf_op jit(solution)/shard_map/ppermute | solution.py:17
  211.5 4.9 %fusion.24 = f32[9,128,1024]{1,2,0:T(8,128)} fusion(bf16[9,128,1024]{2,1,0:T(8,128)(2,1)} %gather_fusion.1, pred[9]{0:T(512)(128)(4,1)S(1)} %copy-done.31, bf16[1,9,128,128]{3,2,1,0:T(8,128)(2,1)S(1)} %copy-done), kind=kOutput, calls=%fused_computation.43 | convolution fusion | flops 303169536 | bytes 7372809 | tf_op jit(solution)/shard_map/kij,kjw->kiw/dot_general | solution.py:60
  216.3 8.1 %copy.71 = f32[9,128,1024]{2,0,1:T(8,128)} copy(f32[9,128,1024]{1,2,0:T(8,128)} %fusion.24) | data formatting | bytes 9437184 | tf_op jit(solution)/shard_map/kij,kjw->kiw/dot_general | solution.py:60
  224.4 6.7 %fusion.113 = bf16[3,128,1024]{2,0,1:T(4,128)(2,1)S(1)} fusion(f32[9,128,1024]{2,0,1:T(8,128)} %copy.71, s32[9]{0:T(128)S(1)} %bitcast.258), kind=kOutput, calls=%fused_computation.177 | convolution fusion | flops 42467356 | bytes 5505060 | tf_op jit(solution)/shard_map/rk,kiw->riw/dot_general | solution.py:63
  235.9 5.8 %collective-permute-start.4 = (bf16[128,1024]{1,0:T(8,128)(2,1)S(1)}, bf16[128,1024]{1,0:T(8,128)(2,1)S(1)}, u32[]{:S(2)}, u32[]{:S(2)}) collective-permute-start(bf16[128,1024]{1,0:T(8,128)(2,1)S(1)} %get-tuple-element.70), channel_id=1, source_target_pairs={{0,12},{4,0},{8,4},{12,8},{1,13},{5,1},{9,5},{13,9},{2,14},{6,2},{... | collective-permute-start | bytes 786440 | tf_op jit(solution)/shard_map/ppermute | solution.py:17
  248.5 6.1 %collective-permute-done.5 = bf16[128,1024]{1,0:T(8,128)(2,1)S(1)} collective-permute-done((bf16[128,1024]{1,0:T(8,128)(2,1)S(1)}, bf16[128,1024]{1,0:T(8,128)(2,1)S(1)}, u32[]{:S(2)}, u32[]{:S(2)}) %collective-permute-start.5) | collective-permute-done | bytes 262176 | tf_op jit(solution)/shard_map/ppermute | solution.py:17
  254.6 8.9 %collective-permute-done.6 = bf16[128,1024]{1,0:T(8,128)(2,1)S(1)} collective-permute-done((bf16[128,1024]{1,0:T(8,128)(2,1)S(1)}, bf16[128,1024]{1,0:T(8,128)(2,1)S(1)}, u32[]{:S(2)}, u32[]{:S(2)}) %collective-permute-start.6) | collective-permute-done | bytes 262176 | tf_op jit(solution)/shard_map/ppermute | solution.py:17
  268.6 4.9 %fusion.27 = f32[9,128,1024]{1,2,0:T(8,128)} fusion(bf16[9,128,1024]{2,1,0:T(8,128)(2,1)} %gather_fusion.3, pred[9]{0:T(512)(128)(4,1)S(1)} %copy-done.32, bf16[1,9,128,128]{3,2,1,0:T(8,128)(2,1)S(1)} %copy-done), kind=kOutput, calls=%fused_computation.44 | convolution fusion | flops 303169536 | bytes 7372809 | tf_op jit(solution)/shard_map/kij,kjw->kiw/dot_general | solution.py:60
  273.4 8.1 %copy.74 = f32[9,128,1024]{2,0,1:T(8,128)} copy(f32[9,128,1024]{1,2,0:T(8,128)} %fusion.27) | data formatting | bytes 9437184 | tf_op jit(solution)/shard_map/kij,kjw->kiw/dot_general | solution.py:60
  281.5 6.7 %convolution_convert_fusion.1 = bf16[3,128,1024]{2,0,1:T(4,128)(2,1)S(1)} fusion(f32[9,128,1024]{2,0,1:T(8,128)} %copy.74, s32[9]{0:T(128)S(1)} %bitcast.259), kind=kOutput, calls=%fused_computation.63 | convolution fusion | flops 42860572 | bytes 5505060 | tf_op jit(solution)/shard_map/rk,kiw->riw/dot_general | solution.py:63
  293.2 87.6 %all-reduce.4.cloned.1.call-done = (f32[2,128,128]{1,2,0:T(8,128)}, f32[2,128,128]{1,2,0:T(8,128)}, f32[3,128,128]{2,1,0:T(8,128)}) async-done(((f32[2,128,128]{1,2,0:T(8,128)}, f32[2,128,128]{1,2,0:T(8,128)}, f32[3,128,128]{2,1,0:T(8,128)}), (f32[2,128,128]{1,2,0:T(8,128)}, f32[2,128,128]{1,2,0:T(8,128)}, f32[3,128,128]{2,1,0:T(8,128)})) %all-reduce.4.cloned.1.call-update) | async-done | bytes 458768 | tf_op jit(solution)/shard_map/psum | solution.py:232
  (186 shorter events, 112.0 us)
Async XLA Ops:
  7.2 373.7 %all-reduce.4.cloned.1.call-start = ((), (), s32[]{:S(2)}) async-start(), calls=%async_computation | async-start | bytes 917504 | tf_op jit(solution)/shard_map/psum | solution.py:232
  14.4 8.1 %copy-start.26 = (s32[1,9]{1,0:T(1,128)S(1)}, s32[1,9]{1,0:T(1,128)}, u32[]{:S(2)}) copy-start(s32[1,9]{1,0:T(1,128)} %param.28) | copy-start | bytes 112
  32.5 10.4 %copy-start.1 = (bf16[384,1,8,128]{3,2,1,0:T(8,128)(2,1)S(1)}, bf16[384,1,8,128]{3,2,1,0:T(8,128)(2,1)}, u32[]{:S(2)}) copy-start(bf16[384,1,8,128]{3,2,1,0:T(8,128)(2,1)} %param.20) | copy-start | bytes 2359300
  32.5 11.4 %copy-start.24 = (s32[1,3,128]{2,0,1:T(1,128)S(1)}, s32[1,3,128]{2,0,1:T(1,128)}, u32[]{:S(2)}) copy-start(s32[1,3,128]{2,0,1:T(1,128)} %param.30) | copy-start | bytes 4612
  32.6 18.8 %collective-permute-start.7 = (bf16[128,1024]{1,0:T(8,128)(2,1)S(1)}, bf16[128,1024]{1,0:T(8,128)(2,1)}, u32[]{:S(2)}, u32[]{:S(2)}) collective-permute-start(bf16[128,1024]{1,0:T(8,128)(2,1)S(1)} %bitcast.241), channel_id=1, source_target_pairs={{0,4},{4,8},{8,12},{12,0},{1,5},{5,9},{9,13},{13,1},{2,6},{6,10},{... | collective-permute-start | bytes 786440 | tf_op jit(solution)/shard_map/ppermute | solution.py:17
  35.7 15.6 %collective-permute-start.8 = (bf16[128,1024]{1,0:T(8,128)(2,1)S(1)}, bf16[128,1024]{1,0:T(8,128)(2,1)}, u32[]{:S(2)}, u32[]{:S(2)}) collective-permute-start(bf16[128,1024]{1,0:T(8,128)(2,1)S(1)} %bitcast.242), channel_id=1, source_target_pairs={{0,12},{4,0},{8,4},{12,8},{1,13},{5,1},{9,5},{13,9},{2,14},{6,2},{... | collective-permute-start | bytes 786440 | tf_op jit(solution)/shard_map/ppermute | solution.py:17
  37.9 23.0 %collective-permute-start.9 = (bf16[128,1024]{1,0:T(8,128)(2,1)S(1)}, bf16[128,1024]{1,0:T(8,128)(2,1)}, u32[]{:S(2)}, u32[]{:S(2)}) collective-permute-start(bf16[128,1024]{1,0:T(8,128)(2,1)S(1)} %bitcast.243), channel_id=1, source_target_pairs={{0,8},{4,12},{8,0},{12,4},{1,9},{5,13},{9,1},{13,5},{2,10},{6,14},... | collective-permute-start | bytes 786440 | tf_op jit(solution)/shard_map/ppermute | solution.py:17
  39.0 97.2 %collective-permute-start = (bf16[384,1,8,128]{3,2,1,0:T(8,128)(2,1)S(1)}, bf16[384,1,8,128]{3,2,1,0:T(8,128)(2,1)S(1)}, u32[]{:S(2)}, u32[]{:S(2)}) collective-permute-start(bf16[384,1,8,128]{3,2,1,0:T(8,128)(2,1)S(1)} %copy-done.2), channel_id=1, source_target_pairs={{0,2},{1,3},{4,6},{5,7},{8,10},{9,11},{12,14},{13,15},{16,18},{17,... | collective-permute-start | bytes 2359304 | tf_op jit(solution)/shard_map/ppermute | solution.py:23
  43.8 18.3 %copy-start.30 = (s32[384]{0:T(512)}, s32[384]{0:T(512)S(1)}, u32[]{:S(2)}) copy-start(s32[384]{0:T(512)S(1)} %fusion.111) | copy-start | bytes 4612
  82.5 8.1 %copy-start.27 = (s32[1,9]{1,0:T(1,128)S(1)}, s32[1,9]{1,0:T(1,128)}, u32[]{:S(2)}) copy-start(s32[1,9]{1,0:T(1,128)} %param.28) | copy-start | bytes 112
  100.6 11.1 %collective-permute-start.10 = (bf16[128,1024]{1,0:T(8,128)(2,1)S(1)}, bf16[128,1024]{1,0:T(8,128)(2,1)S(1)}, u32[]{:S(2)}, u32[]{:S(2)}) collective-permute-start(bf16[128,1024]{1,0:T(8,128)(2,1)S(1)} %bitcast.244), channel_id=1, source_target_pairs={{0,4},{4,8},{8,12},{12,0},{1,5},{5,9},{9,13},{13,1},{2,6},{6,10},{... | collective-permute-start | bytes 786440 | tf_op jit(solution)/shard_map/ppermute | solution.py:17
  100.7 16.4 %collective-permute-start.11 = (bf16[128,1024]{1,0:T(8,128)(2,1)S(1)}, bf16[128,1024]{1,0:T(8,128)(2,1)S(1)}, u32[]{:S(2)}, u32[]{:S(2)}) collective-permute-start(bf16[128,1024]{1,0:T(8,128)(2,1)S(1)} %bitcast.245), channel_id=1, source_target_pairs={{0,12},{4,0},{8,4},{12,8},{1,13},{5,1},{9,5},{13,9},{2,14},{6,2},{... | collective-permute-start | bytes 786440 | tf_op jit(solution)/shard_map/ppermute | solution.py:17
  104.8 20.3 %collective-permute-start.12 = (bf16[128,1024]{1,0:T(8,128)(2,1)S(1)}, bf16[128,1024]{1,0:T(8,128)(2,1)S(1)}, u32[]{:S(2)}, u32[]{:S(2)}) collective-permute-start(bf16[128,1024]{1,0:T(8,128)(2,1)S(1)} %bitcast.246), channel_id=1, source_target_pairs={{0,8},{4,12},{8,0},{12,4},{1,9},{5,13},{9,1},{13,5},{2,10},{6,14},... | collective-permute-start | bytes 786440 | tf_op jit(solution)/shard_map/ppermute | solution.py:17
  185.8 13.2 %collective-permute-start.1 = (bf16[128,1024]{1,0:T(8,128)(2,1)S(1)}, bf16[128,1024]{1,0:T(8,128)(2,1)S(1)}, u32[]{:S(2)}, u32[]{:S(2)}) collective-permute-start(bf16[128,1024]{1,0:T(8,128)(2,1)S(1)} %get-tuple-element.73), channel_id=1, source_target_pairs={{0,12},{4,0},{8,4},{12,8},{1,13},{5,1},{9,5},{13,9},{2,14},{6,2},{... | collective-permute-start | bytes 786440 | tf_op jit(solution)/shard_map/ppermute | solution.py:17
  185.9 13.1 %collective-permute-start.2 = (bf16[128,1024]{1,0:T(8,128)(2,1)S(1)}, bf16[128,1024]{1,0:T(8,128)(2,1)S(1)}, u32[]{:S(2)}, u32[]{:S(2)}) collective-permute-start(bf16[128,1024]{1,0:T(8,128)(2,1)S(1)} %get-tuple-element.75), channel_id=1, source_target_pairs={{0,4},{4,8},{8,12},{12,0},{1,5},{5,9},{9,13},{13,1},{2,6},{6,10},{... | collective-permute-start | bytes 786440 | tf_op jit(solution)/shard_map/ppermute | solution.py:17
  187.9 18.5 %collective-permute-start.3 = (bf16[128,1024]{1,0:T(8,128)(2,1)S(1)}, bf16[128,1024]{1,0:T(8,128)(2,1)S(1)}, u32[]{:S(2)}, u32[]{:S(2)}) collective-permute-start(bf16[128,1024]{1,0:T(8,128)(2,1)S(1)} %get-tuple-element.74), channel_id=1, source_target_pairs={{0,8},{4,12},{8,0},{12,4},{1,9},{5,13},{9,1},{13,5},{2,10},{6,14},... | collective-permute-start | bytes 786440 | tf_op jit(solution)/shard_map/ppermute | solution.py:17
  189.6 195.4 %collective-permute-start.13 = (bf16[384,1,8,128]{3,2,0,1:T(8,128)(2,1)}, bf16[384,1,8,128]{3,2,0,1:T(8,128)(2,1)}, u32[]{:S(2)}, u32[]{:S(2)}) collective-permute-start(bf16[384,1,8,128]{3,2,0,1:T(8,128)(2,1)} %fusion.42), channel_id=1, source_target_pairs={{2,0},{3,1},{6,4},{7,5},{10,8},{11,9},{14,12},{15,13},{18,16},{19,... | collective-permute-start | bytes 2359304 | tf_op jit(solution)/shard_map/ppermute | solution.py:23
  216.3 8.1 %copy-start.28 = (s32[1,9]{1,0:T(1,128)S(1)}, s32[1,9]{1,0:T(1,128)}, u32[]{:S(2)}) copy-start(s32[1,9]{1,0:T(1,128)} %param.27) | copy-start | bytes 112
  235.9 12.6 %collective-permute-start.4 = (bf16[128,1024]{1,0:T(8,128)(2,1)S(1)}, bf16[128,1024]{1,0:T(8,128)(2,1)S(1)}, u32[]{:S(2)}, u32[]{:S(2)}) collective-permute-start(bf16[128,1024]{1,0:T(8,128)(2,1)S(1)} %get-tuple-element.70), channel_id=1, source_target_pairs={{0,12},{4,0},{8,4},{12,8},{1,13},{5,1},{9,5},{13,9},{2,14},{6,2},{... | collective-permute-start | bytes 786440 | tf_op jit(solution)/shard_map/ppermute | solution.py:17
  241.8 12.8 %collective-permute-start.5 = (bf16[128,1024]{1,0:T(8,128)(2,1)S(1)}, bf16[128,1024]{1,0:T(8,128)(2,1)S(1)}, u32[]{:S(2)}, u32[]{:S(2)}) collective-permute-start(bf16[128,1024]{1,0:T(8,128)(2,1)S(1)} %get-tuple-element.72), channel_id=1, source_target_pairs={{0,4},{4,8},{8,12},{12,0},{1,5},{5,9},{9,13},{13,1},{2,6},{6,10},{... | collective-permute-start | bytes 786440 | tf_op jit(solution)/shard_map/ppermute | solution.py:17
  242.0 21.5 %collective-permute-start.6 = (bf16[128,1024]{1,0:T(8,128)(2,1)S(1)}, bf16[128,1024]{1,0:T(8,128)(2,1)S(1)}, u32[]{:S(2)}, u32[]{:S(2)}) collective-permute-start(bf16[128,1024]{1,0:T(8,128)(2,1)S(1)} %get-tuple-element.71), channel_id=1, source_target_pairs={{0,8},{4,12},{8,0},{12,4},{1,9},{5,13},{9,1},{13,5},{2,10},{6,14},... | collective-permute-start | bytes 786440 | tf_op jit(solution)/shard_map/ppermute | solution.py:17
  273.4 8.1 %copy-start.29 = (s32[1,9]{1,0:T(1,128)S(1)}, s32[1,9]{1,0:T(1,128)}, u32[]{:S(2)}) copy-start(s32[1,9]{1,0:T(1,128)} %param.27) | copy-start | bytes 112
  290.5 94.5 %copy-start.22 = (bf16[2,128,128]{2,1,0:T(8,128)(2,1)S(1)}, bf16[2,128,128]{2,1,0:T(8,128)(2,1)}, u32[]{:S(2)}) copy-start(bf16[2,128,128]{2,1,0:T(8,128)(2,1)} %param.22) | copy-start | bytes 196612
  293.2 91.8 %copy-start.4 = (bf16[3072,128]{1,0:T(8,128)(2,1)S(1)}, bf16[3072,128]{1,0:T(8,128)(2,1)}, u32[]{:S(2)}) copy-start(bf16[3072,128]{1,0:T(8,128)(2,1)} %get-tuple-element.58) | copy-start | bytes 2359300
  (32 other events, 86.8 us)
Sparse Core Ops, SparseCore 0:
  290.6 90.2 all-reduce.3
where the time goes:
time: 402 us; the launch traced here: 395 us
  waiting for transfers between devices  143 us (36%)
  matrix products  80.5 us (20%)
  local copies, waits for them, and re-layouts  72 us (18%)
  blocking collectives  30.8 us (8%)
  other arithmetic  29.4 us (7%)
  starting transfers between devices  24.6 us (6%)
  between operations  15 us (4%)
    psum x1, waiting for transfers between devices, on_device(): lax.psum((weight_filter, weight_gate, bias_filter, bias_gate, weight_diff...  87.6 us
    ppermute x12, waiting for transfers between devices, passed_along(): return lax.ppermute(value, axis, pairs)  55.2 us
    psum x1, blocking collectives, on_device(): lax.psum((weight_filter, weight_gate, bias_filter, bias_gate, weight_diff...  30.8 us
    ppermute x12, starting transfers between devices, passed_along(): return lax.ppermute(value, axis, pairs)  19.2 us
    dot_general x2, matrix products, gather_tiles(): jnp.einsum('rk,kiw->riw', selector, products, precision=lax.Precision.HIG...  17.1 us
    dot_general x2, local copies, waits for them, and re-layouts, gather_tiles(): jnp.einsum('kji,kjw->kiw', tile_values, picked, preferred_element_type=jn...  16.2 us
    dot_general x2, local copies, waits for them, and re-layouts, spread_tiles(): jnp.einsum('kij,kjw->kiw', tile_values, picked, preferred_element_type=jn...  16.2 us
    dot_general x2, matrix products, spread_tiles(): jnp.einsum('rk,kiw->riw', selector, products, precision=lax.Precision.HIG...  13.4 us
  transfers between devices with their start and end apart: 15, of which 10 were waited for; matrix products, arithmetic and copies ran while one was open for 34% of the time, Pallas kernels for 0%

commit v1 on v0

v1 whole, which is shorter than its diff:
```python
import functools
import math

import jax
import jax.numpy as jnp
from jax import lax
from jax.experimental import pallas as pl
from jax.experimental.pallas import tpu as pltpu
from jax.sharding import PartitionSpec as P

DILATION_FRAMES = 8
STEPS = (1, -1, 2)
MESH = pl.DeviceIdType.MESH
WIDE = 256
BF = jnp.bfloat16
F32 = jnp.float32


def mm(a, b):
    return lax.dot_general(a, b, (((1,), (0,)), ((), ())), preferred_element_type=F32)


def mm_nt(a, b):
    return lax.dot_general(a, b, (((1,), (1,)), ((), ())), preferred_element_type=F32)


def mm_tn(a, b):
    return lax.dot_general(a, b, (((0,), (0,)), ((), ())), preferred_element_type=F32)


def kernel(
    seg_n, tm_n, scale,
    ser, cot, wf, wg, bf, bg, wd, bd, trow, tcol, tval, snodes, scount,
    out, gs, fin1, fin2,
    prev, ops_f, ops_b, pick, give, wblk,
    acc, act_f, act_g, hid, hop1, delayed_out, delayed_in,
    snd, rcv, wacc, dacc, bacc, cacc,
    red1, red2, ra1, rb1, rc1, sa1, sb1, ra2, rb2, rc2, sa2, sb2,
    tm_s, tm_r, ex_s, ex_r, dl_s, dl_r, ar_s, ar_r,
):
    p = lax.axis_index("seg")
    t = lax.axis_index("tm")
    rep = lax.axis_index("rep")
    chunks, nodes, _ = ser.shape
    cap = 128
    ch = 128

    barrier = pltpu.get_barrier_semaphore()
    for k in range(1, seg_n):
        pl.semaphore_signal(barrier, inc=1, device_id={"seg": lax.rem(p + k, seg_n)}, device_id_type=MESH)
    for k in range(1, tm_n):
        pl.semaphore_signal(barrier, inc=1, device_id={"tm": lax.rem(t + k, tm_n)}, device_id_type=MESH)
    pl.semaphore_signal(barrier, inc=1, device_id={"rep": 1 - rep}, device_id_type=MESH)
    pl.semaphore_wait(barrier, seg_n - 1 + tm_n - 1 + 1)

    def series_copy(c):
        return pltpu.make_async_remote_copy(
            src_ref=ser.at[c], dst_ref=prev.at[c], send_sem=tm_s.at[c], recv_sem=tm_r.at[c],
            device_id={"tm": lax.rem(t + 1, tm_n)}, device_id_type=MESH)

    def delayed_copy(c):
        return pltpu.make_async_remote_copy(
            src_ref=delayed_out.at[c], dst_ref=delayed_in.at[c], send_sem=dl_s.at[c], recv_sem=dl_r.at[c],
            device_id={"tm": lax.rem(t + tm_n - 1, tm_n)}, device_id_type=MESH)

    def halo_copy(e, c, j):
        step = STEPS[j] if e % 2 == 0 else -STEPS[j]
        return pltpu.make_async_remote_copy(
            src_ref=snd.at[e, c, j], dst_ref=rcv.at[e, c, j],
            send_sem=ex_s.at[e, c, j], recv_sem=ex_r.at[e, c, j],
            device_id={"seg": lax.rem(p + step + seg_n, seg_n)}, device_id_type=MESH)

    @pl.when(t < tm_n - 1)
    def _():
        for c in range(chunks):
            series_copy(c).start()

    @pl.when(t == 0)
    def _():
        prev[...] = jnp.zeros_like(prev)

    rows_n, cols_n, tiles_n = nodes // 128, nodes // 128 + 3, tval.shape[0]
    for r in range(rows_n):
        for c in range(cols_n):
            total = jnp.zeros((128, 128), F32)
            for k in range(tiles_n):
                if k < rows_n and (r != k or c != k):
                    continue
                if rows_n <= k < cols_n and c != k:
                    continue
                hit = jnp.where(trow[0, k] == r, 1.0, 0.0) * jnp.where(tcol[0, k] == c, 1.0, 0.0)
                total = total + hit * tval[k].astype(F32)
            ops_f[r * 128:(r + 1) * 128, c * 128:(c + 1) * 128] = total.astype(BF)
            ops_b[c * 128:(c + 1) * 128, r * 128:(r + 1) * 128] = total.T.astype(BF)
    node_ids = lax.broadcasted_iota(jnp.int32, (nodes, cap), 0)
    slot_ids = lax.broadcasted_iota(jnp.int32, (nodes, cap), 1)
    for j in range(3):
        here = jnp.where(node_ids == snodes[j:j + 1, :], 1.0, 0.0)
        live = jnp.where(slot_ids < scount[0, j], 1.0, 0.0)
        hot = here * live
        give[:, j * cap:(j + 1) * cap] = hot.astype(BF)
        pick[j * cap:(j + 1) * cap, :] = hot.T.astype(BF)
    wblk[...] = jnp.zeros_like(wblk)
    for i in range(2):
        lo, hi = i * ch, (i + 1) * ch
        for k in range(2):
            wblk[k, lo:hi, lo:hi] = wf[k]
            wblk[2 + k, lo:hi, lo:hi] = wg[k]
        for k in range(3):
            wblk[4 + k, lo:hi, lo:hi] = wd[k]
    wacc[...] = jnp.zeros_like(wacc)
    dacc[...] = jnp.zeros_like(dacc)
    bacc[...] = jnp.zeros_like(bacc)
    cacc[...] = jnp.zeros_like(cacc)
    red1[...] = jnp.zeros_like(red1)
    red2[...] = jnp.zeros_like(red2)
    ones = jnp.ones((8, nodes), BF)

    def put(e, c, rows):
        for j in range(3):
            snd[e, c, j] = rows[j * cap:(j + 1) * cap]
            halo_copy(e, c, j).start()

    def back_one(c, _):
        g = cot[c]
        up = mm_nt(g, wblk[6]).astype(BF)
        put(0, c, mm(ops_b[nodes:, :], up).astype(BF))
        acc[c] = mm(ops_b[:nodes, :], up) + mm_nt(g, wblk[5])
        return 0

    lax.fori_loop(0, chunks, back_one, 0)

    bf2 = jnp.concatenate([bf[...], bf[...]], axis=1)
    bg2 = jnp.concatenate([bg[...], bg[...]], axis=1)
    bd2 = jnp.concatenate([bd[...], bd[...]], axis=1)

    def fore_one(c, _):
        @pl.when(t > 0)
        def _():
            series_copy(c).wait_recv()

        before, now = prev[c], ser[c]
        a = jnp.tanh(mm(before, wblk[0]) + mm(now, wblk[1]) + bf2)
        act_f[c] = a
        s = jax.nn.sigmoid(mm(before, wblk[2]) + mm(now, wblk[3]) + bg2)
        act_g[c] = s
        h = (a * s).astype(BF)
        hid[c] = h
        put(1, c, mm(pick[...], h).astype(BF))
        return 0

    lax.fori_loop(0, chunks, fore_one, 0)

    def arrived(e, c):
        for j in range(3):
            halo_copy(e, c, j).wait_recv()
        return rcv[e, c].reshape(3 * cap, WIDE)

    def back_two(c, _):
        got = arrived(0, c)
        up = (acc[c] + mm(give[...], got)).astype(BF)
        put(2, c, mm(ops_b[nodes:, :], up).astype(BF))
        acc[c] = mm(ops_b[:nodes, :], up) + mm_nt(cot[c], wblk[4])
        return 0

    lax.fori_loop(0, chunks, back_two, 0)

    def fore_two(c, _):
        got = arrived(1, c)
        h = (mm(ops_f[:, :nodes], hid[c]) + mm(ops_f[:, nodes:], got)).astype(BF)
        hop1[c] = h
        put(3, c, mm(pick[...], h).astype(BF))
        return 0

    lax.fori_loop(0, chunks, fore_two, 0)

    def back_three(c, _):
        got = arrived(2, c)
        gh = acc[c] + mm(give[...], got)
        a, s = act_f[c], act_g[c]
        gf = (gh * s * (1.0 - a * a)).astype(BF)
        gg = (gh * a * (s * (1.0 - s))).astype(BF)
        delayed_out[c] = (mm_nt(gf, wblk[0]) + mm_nt(gg, wblk[2])).astype(BF)

        @pl.when(t > 0)
        def _():
            delayed_copy(c).start()

        g = cot[c]
        acc[c] = g.astype(F32) + mm_nt(gf, wblk[1]) + mm_nt(gg, wblk[3])
        before, now, h, h1 = prev[c], ser[c], hid[c], hop1[c]
        for i in range(2):
            lo, hi = i * ch, (i + 1) * ch
            right = jnp.concatenate([gf[:, lo:hi], gg[:, lo:hi]], axis=1)
            left = jnp.concatenate([before[:, lo:hi], now[:, lo:hi]], axis=1)
            wacc[...] += mm_tn(left, right)
            dacc[...] += mm_tn(jnp.concatenate([h[:, lo:hi], h1[:, lo:hi]], axis=1), g[:, lo:hi])
            bacc[...] += mm(ones, right)
            cacc[...] += mm(ones, g[:, lo:hi])
        return 0

    lax.fori_loop(0, chunks, back_three, 0)

    red1[0:256, :] = wacc[:, 0:128]
    red1[256:512, :] = wacc[:, 128:256]
    red1[512:768, :] = dacc[...]
    rid = lax.broadcasted_iota(jnp.int32, (8, 128), 0)
    red1[768:776, :] = jnp.where(
        rid == 0, bacc[:, 0:128], jnp.where(rid == 1, bacc[:, 128:256], cacc[...]))

    def all_sum(base, red, ra, rb, rc, sa, sb, fin):
        half = red.shape[0] // 2
        part = half // tm_n
        mine = pl.multiple_of(rep * half, 8)
        theirs = pl.multiple_of((1 - rep) * half, 8)
        one = pltpu.make_async_remote_copy(
            src_ref=red.at[pl.ds(theirs, half)], dst_ref=ra,
            send_sem=ar_s.at[base], recv_sem=ar_r.at[base],
            device_id={"rep": 1 - rep}, device_id_type=MESH)
        one.start()
        one.wait()
        sa[...] = red[pl.ds(mine, half), :] + ra[...]
        sends = []
        for k in range(1, tm_n):
            o = lax.rem(t + k, tm_n)
            sends.append(pltpu.make_async_remote_copy(
                src_ref=sa.at[pl.ds(pl.multiple_of(o * part, 8), part)], dst_ref=rb.at[k - 1],
                send_sem=ar_s.at[base + k], recv_sem=ar_r.at[base + k],
                device_id={"tm": o}, device_id_type=MESH))
            sends[-1].start()
        s = sa[pl.ds(pl.multiple_of(t * part, 8), part), :]
        for k in range(1, tm_n):
            sends[k - 1].wait()
            s = s + rb[k - 1]
        sb[...] = s
        rc[p] = s
        at = base + tm_n
        sends = []
        for k in range(1, seg_n):
            sends.append(pltpu.make_async_remote_copy(
                src_ref=sb, dst_ref=rc.at[p],
                send_sem=ar_s.at[at + k], recv_sem=ar_r.at[at + k],
                device_id={"seg": lax.rem(p + k, seg_n)}, device_id_type=MESH))
            sends[-1].start()
        for copy in sends:
            copy.wait()
        s = rc[0]
        for k in range(1, seg_n):
            s = s + rc[k]
        spot = pl.multiple_of(rep * half + t * part, 8)
        fin[pl.ds(spot, part), :] = s * scale
        at = at + seg_n
        sends = []
        for k in range(1, tm_n):
            sends.append(pltpu.make_async_remote_copy(
                src_ref=fin.at[pl.ds(spot, part)], dst_ref=fin.at[pl.ds(spot, part)],
                send_sem=ar_s.at[at + k], recv_sem=ar_r.at[at + k],
                device_id={"tm": lax.rem(t + k, tm_n)}, device_id_type=MESH))
            sends[-1].start()
        for copy in sends:
            copy.wait()
        at = at + tm_n
        last = pltpu.make_async_remote_copy(
            src_ref=fin.at[pl.ds(mine, half)], dst_ref=fin.at[pl.ds(mine, half)],
            send_sem=ar_s.at[at], recv_sem=ar_r.at[at],
            device_id={"rep": 1 - rep}, device_id_type=MESH)
        last.start()
        last.wait()

    all_sum(0, red1, ra1, rb1, rc1, sa1, sb1, fin1)

    def fore_three(c, _):
        got = arrived(3, c)
        h, h1, g = hid[c], hop1[c], cot[c]
        h2 = (mm(ops_f[:, :nodes], h1) + mm(ops_f[:, nodes:], got)).astype(BF)
        total = mm(h, wblk[4]) + mm(h1, wblk[5]) + mm(h2, wblk[6]) + bd2
        out[c] = (ser[c].astype(F32) + total).astype(BF)
        for i in range(2):
            lo, hi = i * ch, (i + 1) * ch
            red2[...] += mm_tn(h2[:, lo:hi], g[:, lo:hi])
        return 0

    lax.fori_loop(0, chunks, fore_three, 0)

    def series_grad(c, _):
        @pl.when(t < tm_n - 1)
        def _():
            delayed_copy(c).wait_recv()
            gs[c] = (acc[c] + delayed_in[c].astype(F32)).astype(BF)

        @pl.when(t == tm_n - 1)
        def _():
            gs[c] = acc[c].astype(BF)

        return 0

    lax.fori_loop(0, chunks, series_grad, 0)
    all_sum(2 * tm_n + seg_n + 1, red2, ra2, rb2, rc2, sa2, sb2, fin2)

    def drain(c, _):
        @pl.when(t < tm_n - 1)
        def _():
            series_copy(c).wait_send()

        @pl.when(t > 0)
        def _():
            delayed_copy(c).wait_send()

        for e in range(4):
            for j in range(3):
                halo_copy(e, c, j).wait_send()
        return 0

    lax.fori_loop(0, chunks, drain, 0)


def on_device(mesh, series, cotangent, w_filter, w_gate, b_filter, b_gate, w_diff, b_diff,
              tile_row, tile_col, tile_val, send_nodes, send_count):
    nodes, batch, frames, channels = series.shape
    seg_n, tm_n, rep_n = mesh.shape["seg"], mesh.shape["tm"], mesh.shape["rep"]
    chunks = batch * frames * channels // WIDE
    scale = 1.0 / math.sqrt(nodes * batch * frames * seg_n * tm_n * rep_n)
    unit = 16 * tm_n
    r1 = -(-776 // unit) * unit
    r2 = -(-128 // unit) * unit

    def chunked(x):
        return x.reshape(nodes, chunks, WIDE).transpose(1, 0, 2)

    def whole(x):
        return x.transpose(1, 0, 2).reshape(nodes, batch, frames, channels)

    vmem = pl.BlockSpec(memory_space=pltpu.VMEM)
    smem = pl.BlockSpec(memory_space=pltpu.SMEM)
    field = (chunks, nodes, WIDE)

    def sums(r):
        h = r // 2
        q = h // tm_n
        return [
            pltpu.VMEM((h, 128), F32),
            pltpu.VMEM((max(tm_n - 1, 1), q, 128), F32),
            pltpu.VMEM((seg_n, q, 128), F32),
            pltpu.VMEM((h, 128), F32),
            pltpu.VMEM((q, 128), F32),
        ]

    n_ar = 2 * (2 * tm_n + seg_n + 1)
    halo = (4, chunks, 3, 128, WIDE)
    out, gs, fin1, fin2 = pl.pallas_call(
        functools.partial(kernel, seg_n, tm_n, scale),
        out_shape=(
            jax.ShapeDtypeStruct(field, BF),
            jax.ShapeDtypeStruct(field, BF),
            jax.ShapeDtypeStruct((r1, 128), F32),
            jax.ShapeDtypeStruct((r2, 128), F32),
        ),
        in_specs=[vmem] * 8 + [smem, smem, vmem, vmem, smem],
        out_specs=(vmem,) * 4,
        scratch_shapes=[
            pltpu.VMEM(field, BF),
            pltpu.VMEM((nodes, nodes + 384), BF),
            pltpu.VMEM((nodes + 384, nodes), BF),
            pltpu.VMEM((384, nodes), BF),
            pltpu.VMEM((nodes, 384), BF),
            pltpu.VMEM((7, WIDE, WIDE), BF),
            pltpu.VMEM(field, F32),
            pltpu.VMEM(field, F32),
            pltpu.VMEM(field, F32),
            pltpu.VMEM(field, BF),
            pltpu.VMEM(field, BF),
            pltpu.VMEM(field, BF),
            pltpu.VMEM(field, BF),
            pltpu.VMEM(halo, BF),
            pltpu.VMEM(halo, BF),
            pltpu.VMEM((256, 256), F32),
            pltpu.VMEM((256, 128), F32),
            pltpu.VMEM((8, 256), F32),
            pltpu.VMEM((8, 128), F32),
            pltpu.VMEM((r1, 128), F32),
            pltpu.VMEM((r2, 128), F32),
            *sums(r1),
            *sums(r2),
            pltpu.SemaphoreType.DMA((chunks,)),
            pltpu.SemaphoreType.DMA((chunks,)),
            pltpu.SemaphoreType.DMA((4, chunks, 3)),
            pltpu.SemaphoreType.DMA((4, chunks, 3)),
            pltpu.SemaphoreType.DMA((chunks,)),
            pltpu.SemaphoreType.DMA((chunks,)),
            pltpu.SemaphoreType.DMA((n_ar,)),
            pltpu.SemaphoreType.DMA((n_ar,)),
        ],
        compiler_params=pltpu.CompilerParams(
            collective_id=0, has_side_effects=True, vmem_limit_bytes=56 << 20),
    )(
        chunked(series), chunked(cotangent), w_filter, w_gate,
        b_filter.reshape(1, -1), b_gate.reshape(1, -1), w_diff, b_diff.reshape(1, -1),
        tile_row, tile_col, tile_val[0], send_nodes[0], send_count,
    )
    return (
        whole(out),
        whole(gs),
        fin1[0:256].reshape(2, 128, 128),
        fin1[256:512].reshape(2, 128, 128),
        fin1[768],
        fin1[769],
        jnp.concatenate([fin1[512:768], fin2[:128]], axis=0).reshape(3, 128, 128),
        fin1[770],
    )


def solution(mesh):
    field = P(("grp", "seg"), "rep", "tm", None)
    part = ("grp", "seg")
    in_specs = (
        field, field, P(), P(), P(), P(), P(), P(),
        P(part, None), P(part, None), P(part, None, None, None), P(part, None, None), P(part, None),
    )
    out_specs = (
        field, field, P("grp", None, None), P("grp", None, None), P("grp"), P("grp"),
        P("grp", None, None), P("grp"),
    )
    return jax.shard_map(
        functools.partial(on_device, mesh), mesh=mesh, in_specs=in_specs, out_specs=out_specs,
        check_vma=False)
```

time: 402 us -> 144 us (0.36); the launches traced: 395 us -> 143 us
  waiting for transfers between devices: 143 us -> 0 us
  Pallas kernels: 0 us -> 130 us
  matrix products: 80.5 us -> 0 us
  local copies, waits for them, and re-layouts: 72 us -> 11.6 us
  blocking collectives: 30.8 us -> 0 us
  other arithmetic: 29.4 us -> 0.69 us
  starting transfers between devices: 24.6 us -> 0 us
  between operations: 15 us -> 0.7 us
    pallas_call x0 -> x1, Pallas kernels: none -> 130 us  [on_device(): pl.pallas_call(functools.partial(kernel, seg_n, tm_n, scale), out_shape=(...]
    psum x1 -> x0, waiting for transfers between devices: 87.6 us -> none  [on_device(): lax.psum((weight_filter, weight_gate, bias_filter, bias_gate, weight_diff...]
    dot_general x29 -> x0, matrix products: 80.5 us -> none  [the longest x2 17.1 us: gather_tiles(): jnp.einsum('rk,kiw->riw', selector, products, precision=lax.Precision.HIG...]
    ppermute x14 -> x0, waiting for transfers between devices: 55.2 us -> none  [the longest x12 55.2 us: passed_along(): return lax.ppermute(value, axis, pairs)]
    dot_general x5 -> x0, local copies, waits for them, and re-layouts: 32.6 us -> none  [the longest x2 16.2 us: gather_tiles(): jnp.einsum('kji,kjw->kiw', tile_values, picked, preferred_element_type=jn...]
    psum x1 -> x0, blocking collectives: 30.8 us -> none  [on_device(): lax.psum((weight_filter, weight_gate, bias_filter, bias_gate, weight_diff...]
    ppermute x14 -> x0, starting transfers between devices: 24.6 us -> none  [the longest x12 19.2 us: passed_along(): return lax.ppermute(value, axis, pairs)]
    gather x6 -> x0, local copies, waits for them, and re-layouts: 15.9 us -> none  [the longest x2 7.42 us: spread_tiles(): picked = jnp.take(source_blocks, col_list, axis=0)]
  transfers between devices with their start and end apart: 15 -> 0, of which waited for: 10 -> 0; matrix products, arithmetic and copies ran while one was open for 34% -> 0% of each run, Pallas kernels for 0% -> 0%
where the time goes in v1:
time: 144 us; the launch traced here: 143 us
  Pallas kernels  130 us (90%)
  local copies, waits for them, and re-layouts  11.6 us (8%)
    pallas_call x1, Pallas kernels, on_device(): pl.pallas_call(functools.partial(kernel, seg_n, tm_n, scale), out_shape=(...  130 us
    unnamed x15, local copies, waits for them, and re-layouts  6.23 us

profile of v1, /device:TPU:0, one launch (start us, length us, event | category | flops | bytes accessed | tf_op | source)
XLA Modules:
  0.0 143.3 jit_solution(258919910823494756)
XLA Ops:
  0.6 0.0 copy-start.4
  0.6 0.7 copy-done.4
  1.3 0.6 copy.31
  1.9 1.6 %copy.21 = bf16[384,1,8,128]{0,3,2,1:T(8,128)(2,1)S(1)} copy(bf16[384,1,8,128]{3,2,1,0:T(8,128)(2,1)} %param.13) | data formatting | bytes 1572864 | tf_op args[0]
  3.5 0.0 copy-start
  3.5 1.2 copy.22
  4.7 0.0 copy-done
  4.7 0.6 copy.23
  5.2 1.2 copy.24
  6.4 130.3 %shard_map.188 = (bf16[4,384,256]{2,1,0:T(8,128)(2,1)}, bf16[4,384,256]{2,1,0:T(8,128)(2,1)}, f32[800,128]{1,0:T(8,128)}, f32[128,128]{1,0:T(8,128)}) custom-call(bf16[4,384,256]{2,1,0:T(8,128)(2,1)} %bitcast.28, bf16[4,384,256]{2,1,0:T(8,128)(2,1)} %bitcast.29, bf16[2,128,128]{2,1,0:T(8,128)(2,1)} %wf.1, bf16[2,128,128]{2,1,0:T(8,128)(2,1)} %wg.1, ...), custom_call_target="tpu_custom_call" | custom-call | tf_op jit(solution)/shard_map/pallas_call | solution.py:350
  136.7 1.5 %copy.25 = bf16[384,4,256]{0,2,1:T(8,128)(2,1)S(1)} copy(bf16[384,4,256]{2,0,1:T(8,128)(2,1)} %bitcast.31) | data formatting | bytes 1572864 | tf_op jit(solution)/shard_map/transpose | solution.py:331
  138.2 0.0 copy-start.1
  138.2 1.3 copy.27
  139.6 0.0 copy-done.1
  139.6 0.4 copy.26
  139.9 0.0 copy-start.2
  139.9 1.3 copy.28
  141.3 0.0 copy-done.2
  141.3 0.5 slice_bitcast_fusion
  141.8 0.0 copy-start.3
  141.8 0.7 fusion
  142.5 0.1 copy-done.3
  142.7 0.7 pad_maximum_fusion
Async XLA Ops:
  0.6 0.7 copy-start.4
  3.5 1.2 copy-start
  138.2 1.4 copy-start.1
  139.9 1.4 copy-start.2
  141.8 0.8 copy-start.3
